TPU v7x, 1024 devices: a whole 4x4x32 slice. The times are simulated.
1024 devices in a mesh: dp: 32 (over x, z_hi, core), fsdp: 32 (over y, z_lo).
Axes of the slice: x: 4, y: 4, z: 32 (z_hi: 4, z_lo: 8; z = z_hi * 8 + z_lo), core: 2. Of those that a mesh axis runs over, the one named last changes fastest.
Arguments:
- query_in: bfloat16 [229376, 1024], P(('dp', 'fsdp')), may hold values from -32 to 32
- key_in: bfloat16 [229376, 1024], P(('dp', 'fsdp')), may hold values from -32 to 32
- value_in: bfloat16 [229376, 1024], P(('dp', 'fsdp')), may hold values from -6 to 6
- length_plan: int32 [1024, 224], P(('dp', 'fsdp')), may hold values from 0 to 223, each once within a row
- segment_ids: int32 [1024, 224], P(('dp', 'fsdp')), may hold values from 0 to 3, never falling along the last dimension, each value on 1 to 112 neighbouring positions
- out_grad: bfloat16 [229376, 1024], P(('dp', 'fsdp')), may hold values from -6 to 6
- query_gain: float32 [128], replicated, may hold values from 0.7 to 6
- key_gain: float32 [128], replicated, may hold values from 0.7 to 6
Outputs:
- query_grad: bfloat16 [229376, 1024], P(('dp', 'fsdp'))
- key_grad: bfloat16 [229376, 1024], P(('dp', 'fsdp'))
- value_grad: bfloat16 [229376, 1024], P(('dp', 'fsdp'))
- query_gain_grad: float32 [128], replicated
- key_gain_grad: float32 [128], replicated
Inputs may be any that keep to these rules, and one draw needn't show every extreme that they name: `length_plan`: each row is a permutation of 0 to 223. `segment_ids`: within a row the numbers never fall; each utterance piece holds 1 to 112 frames, and one holds exactly 112.
All inputs are finite; a program needn't handle non-finite values.
Results may differ from a plain program's by a relative error of at most 0.01.
The roundings to bfloat16 on the way count: a program that leaves them out, or rounds other values in their place, can miss the bound.
Values may be sent and summed in bfloat16 or wider, within the bound.
No kernel may reach another device: no remote copies, remote signals or barrier semaphores. Data moves between devices by JAX's collectives and lax.ppermute only.
A program may use at most 32 MiB of HBM per device.

v0:
```python
import jax
import jax.numpy as jnp
from jax import lax
from jax.sharding import PartitionSpec as P

HEAD = 128


def normalize(raw, gain):
    frames = raw.shape[0]
    values = raw.astype(jnp.float32).reshape(frames, -1, HEAD)
    inv_rms = lax.rsqrt(jnp.mean(values * values, axis=-1, keepdims=True) + 1e-06)
    unit_vec = values * inv_rms
    return (unit_vec, inv_rms, (unit_vec * gain).astype(jnp.bfloat16))


def norm_back(d_norm, unit_vec, inv_rms, gain):
    d_unit = d_norm * gain
    inner = jnp.mean(d_unit * unit_vec, axis=-1, keepdims=True)
    result = inv_rms * (d_unit - unit_vec * inner)
    return result.reshape(result.shape[0], -1).astype(jnp.bfloat16)


def attend_heads(query_pk, key_pk, value_pk, grad_rows, segment_row, query_gain, key_gain):
    frames = query_pk.shape[0]
    score_scale = HEAD ** (-0.5)
    q_unit, q_inv, q_norm = normalize(query_pk, query_gain)
    k_unit, k_inv, k_norm = normalize(key_pk, key_gain)
    scores = (
        jnp.einsum("thd,shd->hts", q_norm, k_norm, preferred_element_type=jnp.float32) * score_scale
    )
    same_seg = segment_row[:, None] == segment_row[None, :]
    scores = jnp.where(same_seg[None], scores, -jnp.inf)
    row_max = jnp.max(scores, axis=-1, keepdims=True)
    exponent = jnp.exp(scores - row_max)
    attn_probs = exponent / jnp.sum(exponent, axis=-1, keepdims=True)
    value_heads = value_pk.reshape(frames, -1, HEAD)
    grad_heads = grad_rows.reshape(frames, -1, HEAD)
    probs_half = attn_probs.astype(jnp.bfloat16)
    output = jnp.einsum("hts,shd->thd", probs_half, value_heads, preferred_element_type=jnp.float32)
    row_delta = jnp.sum(grad_heads.astype(jnp.float32) * output, axis=-1)
    value_grad = jnp.einsum(
        "hts,thd->shd", probs_half, grad_heads, preferred_element_type=jnp.float32
    )
    value_grad = value_grad.astype(jnp.bfloat16).reshape(frames, -1)
    d_prob = jnp.einsum("thd,shd->hts", grad_heads, value_heads, preferred_element_type=jnp.float32)
    d_score = (attn_probs * (d_prob - row_delta.T[:, :, None]) * score_scale).astype(jnp.bfloat16)
    d_qnorm = jnp.einsum("hts,shd->thd", d_score, k_norm, preferred_element_type=jnp.float32)
    d_knorm = jnp.einsum("hts,thd->shd", d_score, q_norm, preferred_element_type=jnp.float32)
    query_part = jnp.sum(d_qnorm * q_unit, axis=(0, 1))
    key_part = jnp.sum(d_knorm * k_unit, axis=(0, 1))
    query_grad = norm_back(d_qnorm, q_unit, q_inv, query_gain)
    key_grad = norm_back(d_knorm, k_unit, k_inv, key_gain)
    return (query_grad, key_grad, value_grad, query_part, key_part)


def on_device(query_in, key_in, value_in, length_plan, segment_ids, out_grad, query_gain, key_gain):
    frames = query_in.shape[0]
    positions = jnp.arange(frames, dtype=jnp.int32)
    inverse = jnp.zeros((frames,), jnp.int32).at[length_plan[0]].set(positions)
    send_query = query_in[inverse]
    send_key = key_in[inverse]
    send_value = value_in[inverse]
    segment_row = segment_ids[0]
    query_pk, key_pk, value_pk = (
        lax.all_to_all(send_query, "dp", split_axis=0, concat_axis=0, tiled=True),
        lax.all_to_all(send_key, "dp", split_axis=0, concat_axis=0, tiled=True),
        lax.all_to_all(send_value, "dp", split_axis=0, concat_axis=0, tiled=True),
    )
    query_grad, key_grad, value_grad, query_part, key_part = attend_heads(
        query_pk, key_pk, value_pk, out_grad, segment_row, query_gain, key_gain
    )
    query_total, key_total = lax.psum((query_part, key_part), ("dp", "fsdp"))
    return (query_grad, key_grad, value_grad, query_total, key_total)


def solution(mesh):
    in_specs = (
        P(("dp", "fsdp"), None),
        P(("dp", "fsdp"), None),
        P(("dp", "fsdp"), None),
        P(("dp", "fsdp"), None),
        P(("dp", "fsdp"), None),
        P(("dp", "fsdp"), None),
        P(),
        P(),
    )
    out_specs = (
        P(("dp", "fsdp"), None),
        P(("dp", "fsdp"), None),
        P(("dp", "fsdp"), None),
        P(),
        P(),
    )
    return jax.shard_map(
        on_device, mesh=mesh, in_specs=in_specs, out_specs=out_specs, check_vma=False
    )
```

profile of v0, /device:TPU:1, one launch (start us, length us, event | category | flops | bytes accessed | tf_op | source)
XLA Modules:
  0.0 393.6 jit_solution(11603254327852789225)
XLA Ops:
  0.6 0.0 copy-start
  0.6 0.7 compare_select_fusion
  1.4 1.3 scatter_custom_fusion
  2.7 2.5 gather_fusion.1
  5.2 0.0 copy-start.1
  5.2 1.0 all_to_all.20
  6.2 32.4 %all-to-all-start.1 = ((bf16[32,7,1024]{2,1,0:T(8,128)(2,1)}), bf16[32,7,1024]{2,1,0:T(8,128)(2,1)S(1)}, u32[]{:S(2)}, u32[]{:S(2)}) async-start(bf16[32,7,1024]{2,1,0:T(8,128)(2,1)} %all_to_all.20), calls=%async_computation.1 | async-start | bytes 1048576 | tf_op jit(solution)/shard_map/all_to_all | solution.py:67
  38.7 0.0 copy-done.1
  38.7 1.1 gather_fusion
  39.8 0.0 copy-start.2
  39.8 0.9 all_to_all.18
  40.7 51.1 %all-to-all-done.1 = bf16[32,7,1024]{2,1,0:T(8,128)(2,1)S(1)} async-done(((bf16[32,7,1024]{2,1,0:T(8,128)(2,1)}), bf16[32,7,1024]{2,1,0:T(8,128)(2,1)S(1)}, u32[]{:S(2)}, u32[]{:S(2)}) %all-to-all-start.1) | async-done | bytes 458784 | tf_op jit(solution)/shard_map/all_to_all | solution.py:67
  91.8 14.7 %all-to-all-start = ((bf16[32,7,1024]{2,1,0:T(8,128)(2,1)}), bf16[32,7,1024]{2,1,0:T(8,128)(2,1)S(1)}, u32[]{:S(2)}, u32[]{:S(2)}) async-start(bf16[32,7,1024]{2,1,0:T(8,128)(2,1)} %all_to_all.18), calls=%async_computation | async-start | bytes 1048576 | tf_op jit(solution)/shard_map/all_to_all | solution.py:66
  106.5 0.0 copy-done.2
  106.5 1.1 gather_fusion.2
  107.6 0.0 copy-start.7
  107.6 1.0 all_to_all.22
  108.6 52.8 %all-to-all-done = bf16[32,7,1024]{2,1,0:T(8,128)(2,1)S(1)} async-done(((bf16[32,7,1024]{2,1,0:T(8,128)(2,1)}), bf16[32,7,1024]{2,1,0:T(8,128)(2,1)S(1)}, u32[]{:S(2)}, u32[]{:S(2)}) %all-to-all-start) | async-done | bytes 458784 | tf_op jit(solution)/shard_map/all_to_all | solution.py:66
  161.4 11.8 %all-to-all-start.2 = ((bf16[32,7,1024]{2,1,0:T(8,128)(2,1)}), bf16[32,7,1024]{2,1,0:T(8,128)(2,1)S(1)}, u32[]{:S(2)}, u32[]{:S(2)}) async-start(bf16[32,7,1024]{2,1,0:T(8,128)(2,1)} %all_to_all.22), calls=%async_computation.2 | async-start | bytes 1048576 | tf_op jit(solution)/shard_map/all_to_all | solution.py:68
  173.2 0.0 copy-done.7
  173.3 0.1 broadcast_compare_fusion
  173.4 0.5 reshape.129
  173.9 0.0 copy-start.5
  173.9 0.0 copy-start.6
  173.9 0.3 multiply_reduce_fusion.4
  174.2 0.1 copy.60
  174.3 0.5 reshape.128
  174.8 0.3 multiply_reduce_fusion.5
  175.1 0.1 copy.59
  175.2 0.0 copy-done.5
  175.2 0.0 copy-done.6
  175.2 2.2 fusion.27
  177.4 0.0 copy-done
  177.4 2.7 fusion.6
  180.1 37.9 %all-to-all-done.2 = bf16[32,7,1024]{2,1,0:T(8,128)(2,1)S(1)} async-done(((bf16[32,7,1024]{2,1,0:T(8,128)(2,1)}), bf16[32,7,1024]{2,1,0:T(8,128)(2,1)S(1)}, u32[]{:S(2)}, u32[]{:S(2)}) %all-to-all-start.2) | async-done | bytes 458784 | tf_op jit(solution)/shard_map/all_to_all | solution.py:68
  217.9 0.5 reshape.125
  218.5 0.0 copy-start.8
  218.5 2.3 fusion.5
  220.8 0.0 copy-done.8
  220.8 0.5 fusion.2
  221.3 1.8 multiply_reduce_fusion
  223.1 1.5 multiply_reduce_fusion.1
  224.6 166.2 %all-reduce = (f32[128]{0:T(128)}, f32[128]{0:T(128)}) all-reduce(f32[128]{0:T(128)S(1)} %get-tuple-element.7, f32[128]{0:T(128)S(1)} %get-tuple-element.5), channel_id=1, replica_groups=mesh['dp'=32,'fsdp'=32] {'dp','fsdp'}, use_global_device_ids=true, to_apply=%region_9.10 | all-reduce | flops 256 | bytes 2048 | tf_op jit(solution)/shard_map/psum | solution.py:73
  390.8 0.0 copy-start.3
  390.8 0.0 copy-start.4
  390.8 1.3 copy_bitcast_fusion.2
  392.2 0.0 copy-done.3
  392.2 0.0 copy-done.4
  392.2 1.4 copy_bitcast_fusion
  (7 shorter events, 0.0 us)
Async XLA Ops:
  0.6 176.8 %copy-start = (bf16[224,1024]{1,0:T(8,128)(2,1)S(1)}, bf16[224,1024]{1,0:T(8,128)(2,1)}, u32[]{:S(2)}) copy-start(bf16[224,1024]{1,0:T(8,128)(2,1)} %param.13) | copy-start | bytes 1376260
  5.2 33.4 %copy-start.1 = (bf16[224,1024]{1,0:T(8,128)(2,1)S(1)}, bf16[224,1024]{1,0:T(8,128)(2,1)}, u32[]{:S(2)}) copy-start(bf16[224,1024]{1,0:T(8,128)(2,1)} %param.8) | copy-start | bytes 1376260
  6.2 85.6 %all-to-all-start.1 = ((bf16[32,7,1024]{2,1,0:T(8,128)(2,1)}), bf16[32,7,1024]{2,1,0:T(8,128)(2,1)S(1)}, u32[]{:S(2)}, u32[]{:S(2)}) async-start(bf16[32,7,1024]{2,1,0:T(8,128)(2,1)} %all_to_all.20), calls=%async_computation.1 | async-start | bytes 1048576 | tf_op jit(solution)/shard_map/all_to_all | solution.py:67
  39.8 66.8 %copy-start.2 = (bf16[224,1024]{1,0:T(8,128)(2,1)S(1)}, bf16[224,1024]{1,0:T(8,128)(2,1)}, u32[]{:S(2)}) copy-start(bf16[224,1024]{1,0:T(8,128)(2,1)} %param.10) | copy-start | bytes 1376260
  91.8 69.6 %all-to-all-start = ((bf16[32,7,1024]{2,1,0:T(8,128)(2,1)}), bf16[32,7,1024]{2,1,0:T(8,128)(2,1)S(1)}, u32[]{:S(2)}, u32[]{:S(2)}) async-start(bf16[32,7,1024]{2,1,0:T(8,128)(2,1)} %all_to_all.18), calls=%async_computation | async-start | bytes 1048576 | tf_op jit(solution)/shard_map/all_to_all | solution.py:66
  107.6 65.6 %copy-start.7 = (s32[1,224]{1,0:T(1,128)S(1)}, s32[1,224]{1,0:T(1,128)}, u32[]{:S(2)}) copy-start(s32[1,224]{1,0:T(1,128)} %param.12) | copy-start | bytes 2692
  161.4 56.5 %all-to-all-start.2 = ((bf16[32,7,1024]{2,1,0:T(8,128)(2,1)}), bf16[32,7,1024]{2,1,0:T(8,128)(2,1)S(1)}, u32[]{:S(2)}, u32[]{:S(2)}) async-start(bf16[32,7,1024]{2,1,0:T(8,128)(2,1)} %all_to_all.22), calls=%async_computation.2 | async-start | bytes 1048576 | tf_op jit(solution)/shard_map/all_to_all | solution.py:68
  173.9 1.3 copy-start.5
  173.9 1.3 copy-start.6
  218.5 2.3 copy-start.8
  390.8 1.3 copy-start.3
  390.8 1.3 copy-start.4
where the time goes:
time: 394 us
  blocking collectives  166 us (42%)
  waiting for transfers between devices  142 us (36%)
  starting transfers between devices  59 us (15%)
  matrix products  10.9 us (3%)
  local copies, waits for them, and re-layouts  10.6 us (3%)
  other arithmetic  4.24 us (1%)
    psum x1, blocking collectives, on_device(): query_total, key_total = lax.psum((query_part, key_part), ('dp', 'fsdp'))  166 us
    all_to_all x1, waiting for transfers between devices, on_device(): lax.all_to_all(send_query, 'dp', split_axis=0, concat_axis=0, tiled=True)  52.8 us
    all_to_all x1, waiting for transfers between devices, on_device(): lax.all_to_all(send_key, 'dp', split_axis=0, concat_axis=0, tiled=True)  51.1 us
    all_to_all x1, waiting for transfers between devices, on_device(): lax.all_to_all(send_value, 'dp', split_axis=0, concat_axis=0, tiled=True)  37.9 us
    all_to_all x1, starting transfers between devices, on_device(): lax.all_to_all(send_key, 'dp', split_axis=0, concat_axis=0, tiled=True)  32.4 us
    all_to_all x1, starting transfers between devices, on_device(): lax.all_to_all(send_query, 'dp', split_axis=0, concat_axis=0, tiled=True)  14.7 us
    all_to_all x1, starting transfers between devices, on_device(): lax.all_to_all(send_value, 'dp', split_axis=0, concat_axis=0, tiled=True)  11.8 us
  transfers between devices with their start and end apart: 3, of which 3 were waited for; matrix products, arithmetic and copies ran while one was open for 2% of the time, Pallas kernels for 0%

commit v1 on v0

--- a/solution.py
+++ b/solution.py
@@ -54,23 +54,46 @@
     return (query_grad, key_grad, value_grad, query_part, key_part)
 
 
+def plane_and_line_groups():
+    def flat(x, z_hi, core, y, z_lo):
+        return ((x * 4 + z_hi) * 2 + core) * 32 + y * 8 + z_lo
+
+    plane = [
+        [flat(x, z_hi, core, y, z_lo) for x in range(4) for y in range(4) for core in range(2)]
+        for z_hi in range(4)
+        for z_lo in range(8)
+    ]
+    line = [
+        [flat(x, z_hi, core, y, z_lo) for z_hi in range(4) for z_lo in range(8)]
+        for x in range(4)
+        for y in range(4)
+        for core in range(2)
+    ]
+    return plane, line
+
+
+def sum_over_all(part):
+    for groups in plane_and_line_groups():
+        spread = jnp.broadcast_to(part, (len(groups[0]), *part.shape))
+        spread = lax.all_to_all(
+            spread, ("dp", "fsdp"), 0, 0, axis_index_groups=groups, tiled=True
+        )
+        part = jnp.sum(lax.optimization_barrier(spread), axis=0)
+    return part
+
+
 def on_device(query_in, key_in, value_in, length_plan, segment_ids, out_grad, query_gain, key_gain):
-    frames = query_in.shape[0]
+    frames, width = query_in.shape
+    groups = lax.axis_size("dp")
     positions = jnp.arange(frames, dtype=jnp.int32)
     inverse = jnp.zeros((frames,), jnp.int32).at[length_plan[0]].set(positions)
-    send_query = query_in[inverse]
-    send_key = key_in[inverse]
-    send_value = value_in[inverse]
-    segment_row = segment_ids[0]
-    query_pk, key_pk, value_pk = (
-        lax.all_to_all(send_query, "dp", split_axis=0, concat_axis=0, tiled=True),
-        lax.all_to_all(send_key, "dp", split_axis=0, concat_axis=0, tiled=True),
-        lax.all_to_all(send_value, "dp", split_axis=0, concat_axis=0, tiled=True),
+    sends = [source[inverse].reshape(groups, -1, HEAD) for source in (query_in, key_in, value_in)]
+    got = lax.all_to_all(jnp.concatenate(sends, axis=1), "dp", 0, 0, tiled=True)
+    query_pk, key_pk, value_pk = (part.reshape(frames, width) for part in jnp.split(got, 3, axis=1))
+    query_grad, key_grad, value_grad, query_part, key_part = attend_heads(
+        query_pk, key_pk, value_pk, out_grad, segment_ids[0], query_gain, key_gain
     )
-    query_grad, key_grad, value_grad, query_part, key_part = attend_heads(
-        query_pk, key_pk, value_pk, out_grad, segment_row, query_gain, key_gain
-    )
-    query_total, key_total = lax.psum((query_part, key_part), ("dp", "fsdp"))
+    query_total, key_total = sum_over_all(jnp.stack([query_part, key_part]))
     return (query_grad, key_grad, value_grad, query_total, key_total)
 
 

time: 394 us -> 235 us (0.60)
  blocking collectives: 166 us -> 0 us
  waiting for transfers between devices: 142 us -> 150 us
    psum x1 -> x0, blocking collectives: 166 us -> none  [on_device(): query_total, key_total = lax.psum((query_part, key_part), ('dp', 'fsdp'))]
    all_to_all x3, waiting for transfers between devices: 142 us -> 150 us  [the longest x1 126 us: on_device(): got = lax.all_to_all(jnp.concatenate(sends, axis=1), 'dp', 0, 0, tiled=True)]
where the time goes in v1:
time: 235 us
  waiting for transfers between devices  150 us (64%)
  starting transfers between devices  56.3 us (24%)
  local copies, waits for them, and re-layouts  9.88 us (4%)
  matrix products  9.4 us (4%)
  other arithmetic  8.05 us (3%)
    all_to_all x1, waiting for transfers between devices, on_device(): got = lax.all_to_all(jnp.concatenate(sends, axis=1), 'dp', 0, 0, tiled=True)  126 us
    all_to_all x1, starting transfers between devices, on_device(): got = lax.all_to_all(jnp.concatenate(sends, axis=1), 'dp', 0, 0, tiled=True)  32.6 us
    all_to_all x2, waiting for transfers between devices, sum_over_all(): lax.all_to_all(spread, ('dp', 'fsdp'), 0, 0, axis_index_groups=groups, ti...  24.5 us
    all_to_all x2, starting transfers between devices, sum_over_all(): lax.all_to_all(spread, ('dp', 'fsdp'), 0, 0, axis_index_groups=groups, ti...  23.7 us
    gather x3, local copies, waits for them, and re-layouts, on_device(): source[inverse].reshape(groups, -1, HEAD)  4.75 us
  transfers between devices with their start and end apart: 3, of which 3 were waited for; matrix products, arithmetic and copies ran while one was open for 2% of the time, Pallas kernels for 0%

profile of v1, /device:TPU:1, one launch (start us, length us, event | category | flops | bytes accessed | tf_op | source)
XLA Modules:
  0.0 235.0 jit_solution(8786227434871930243)
XLA Ops:
  0.6 0.0 copy-start
  0.6 0.7 compare_select_fusion
  1.4 1.3 scatter_custom_fusion
  2.7 0.0 copy-start.1
  2.7 2.6 %gather_fusion.2 = bf16[224,1024]{1,0:T(8,128)(2,1)S(1)} fusion(bf16[224,1024]{1,0:T(8,128)(2,1)} %param.10, s32[1024]{0:T(1024)S(1)} %pad_clamp_fusion), kind=kCustom, calls=%fused_computation.2 | custom fusion | bytes 918400 | tf_op jit(solution)/shard_map/gather | solution.py:90
  5.3 0.2 reshape.146
  5.5 0.0 copy-done.1
  5.5 0.0 copy-start.2
  5.5 1.1 gather_fusion.1
  6.6 0.2 reshape.145
  6.8 0.0 copy-done.2
  6.8 1.1 gather_fusion
  7.9 0.2 reshape.144
  8.1 1.2 pad_maximum_fusion
  9.3 0.0 copy-start.7
  9.3 32.6 %all-to-all-start = ((bf16[32,168,128]{2,1,0:T(8,128)(2,1)}), bf16[32,168,128]{2,1,0:T(8,128)(2,1)S(1)}, u32[]{:S(2)}, u32[]{:S(2)}) async-start(bf16[32,168,128]{2,1,0:T(8,128)(2,1)} %pad_maximum_fusion), calls=%async_computation | async-start | bytes 2752512 | tf_op jit(solution)/shard_map/all_to_all | solution.py:91
  41.9 0.0 copy-done.7
  41.9 0.1 broadcast_compare_fusion
  42.0 126.0 %all-to-all-done = bf16[32,168,128]{2,1,0:T(8,128)(2,1)S(1)} async-done(((bf16[32,168,128]{2,1,0:T(8,128)(2,1)}), bf16[32,168,128]{2,1,0:T(8,128)(2,1)S(1)}, u32[]{:S(2)}, u32[]{:S(2)}) %all-to-all-start) | async-done | bytes 1376288 | tf_op jit(solution)/shard_map/all_to_all | solution.py:91
  168.0 0.0 copy-start.3
  168.0 0.5 multiply_reduce_fusion.5
  168.6 0.1 rsqrt.25
  168.7 0.1 copy.16
  168.7 0.1 rsqrt.23
  168.8 0.2 copy-done.3
  169.1 0.1 copy.15
  169.1 0.0 copy-start.5
  169.1 0.0 copy-start.6
  169.1 1.5 fusion.27
  170.6 0.0 copy-done.5
  170.6 0.0 copy-done.6
  170.6 2.2 fusion.28
  172.8 0.0 copy-done
  172.8 0.0 copy-start.8
  172.8 2.8 %fusion.6 = bf16[8,28,8,128]{3,2,1,0:T(8,128)(2,1)} fusion(f32[8,224,224]{1,2,0:T(8,128)} %get-tuple-element.17, f32[8,224]{1,0:T(8,128)S(1)} %get-tuple-element.16, bf16[224,1024]{1,0:T(8,128)(2,1)S(1)} %copy-done), kind=kOutput, calls=%fused_computation.18 | convolution fusion | flops 103792640 | bytes 2530304 | tf_op jit(solution)/shard_map/hts,thd->shd/dot_general | solution.py:42
  175.6 0.0 copy-done.8
  175.6 0.6 fusion.5
  176.3 0.5 fusion.2
  176.8 1.8 multiply_reduce_fusion
  178.7 1.4 multiply_reduce_fusion.1
  180.1 0.6 broadcast_in_dim.21
  180.7 6.8 %all-to-all-start.1 = ((f32[32,2,128]{2,1,0:T(2,128)}), f32[32,2,128]{2,1,0:T(2,128)S(1)}, u32[]{:S(2)}, u32[]{:S(2)}) async-start(f32[32,2,128]{2,1,0:T(2,128)} %broadcast_in_dim.21), calls=%async_computation.1 | async-start | bytes 65536 | tf_op jit(solution)/shard_map/all_to_all | solution.py:78
  187.5 0.0 copy-start.4
  187.5 2.5 %copy_bitcast_fusion.1 = bf16[224,1024]{1,0:T(8,128)(2,1)} fusion(f32[224,8,128]{2,1,0:T(8,128)S(1)} %bitcast.71, f32[224,8,128]{2,0,1:T(8,128)} %get-tuple-element.19, f32[224,8]{0,1:T(8,128)S(1)} %broadcast_multiply_fusion, f32[128]{0:T(128)S(1)} %copy-done.5, f32[224,8]{0,1:T(8,128)S(1)} %copy.16), kind=kLoop, calls=%fused_computation.39 | loop fusion | flops 1376256 | bytes 2308608 | tf_op jit(solution)/shard_map/convert_element_type | solution.py:21
  190.1 0.0 copy-done.4
  190.1 0.9 copy.81
  191.0 3.8 %all-to-all-done.1 = f32[32,2,128]{2,1,0:T(2,128)S(1)} async-done(((f32[32,2,128]{2,1,0:T(2,128)}), f32[32,2,128]{2,1,0:T(2,128)S(1)}, u32[]{:S(2)}, u32[]{:S(2)}) %all-to-all-start.1) | async-done | bytes 32800 | tf_op jit(solution)/shard_map/all_to_all | solution.py:78
  194.8 0.6 broadcast_in_dim.22
  195.5 16.9 %all-to-all-start.2 = ((f32[32,2,128]{2,1,0:T(2,128)}), f32[32,2,128]{2,1,0:T(2,128)S(1)}, u32[]{:S(2)}, u32[]{:S(2)}) async-start(f32[32,2,128]{2,1,0:T(2,128)} %broadcast_in_dim.22), calls=%async_computation.2 | async-start | bytes 65536 | tf_op jit(solution)/shard_map/all_to_all | solution.py:78
  212.4 1.3 copy_bitcast_fusion.2
  213.7 20.7 %all-to-all-done.2 = f32[32,2,128]{2,1,0:T(2,128)S(1)} async-done(((f32[32,2,128]{2,1,0:T(2,128)}), f32[32,2,128]{2,1,0:T(2,128)S(1)}, u32[]{:S(2)}, u32[]{:S(2)}) %all-to-all-start.2) | async-done | bytes 32800 | tf_op jit(solution)/shard_map/all_to_all | solution.py:78
  234.5 0.5 slice_bitcast_fusion
  (9 shorter events, 0.1 us)
Async XLA Ops:
  0.6 172.2 %copy-start = (bf16[224,1024]{1,0:T(8,128)(2,1)S(1)}, bf16[224,1024]{1,0:T(8,128)(2,1)}, u32[]{:S(2)}) copy-start(bf16[224,1024]{1,0:T(8,128)(2,1)} %param.13) | copy-start | bytes 1376260
  2.7 2.8 %copy-start.1 = (bf16[224,1024]{1,0:T(8,128)(2,1)S(1)}, bf16[224,1024]{1,0:T(8,128)(2,1)}, u32[]{:S(2)}) copy-start(bf16[224,1024]{1,0:T(8,128)(2,1)} %param.9) | copy-start | bytes 1376260
  5.5 1.3 copy-start.2
  9.3 32.6 %copy-start.7 = (s32[1,224]{1,0:T(1,128)S(1)}, s32[1,224]{1,0:T(1,128)}, u32[]{:S(2)}) copy-start(s32[1,224]{1,0:T(1,128)} %param.12) | copy-start | bytes 2692
  9.3 158.7 %all-to-all-start = ((bf16[32,168,128]{2,1,0:T(8,128)(2,1)}), bf16[32,168,128]{2,1,0:T(8,128)(2,1)S(1)}, u32[]{:S(2)}, u32[]{:S(2)}) async-start(bf16[32,168,128]{2,1,0:T(8,128)(2,1)} %pad_maximum_fusion), calls=%async_computation | async-start | bytes 2752512 | tf_op jit(solution)/shard_map/all_to_all | solution.py:91
  168.0 1.1 copy-start.3
  169.1 1.5 copy-start.5
  169.1 1.5 copy-start.6
  172.8 2.8 %copy-start.8 = (f32[8,224,224]{1,2,0:T(8,128)S(1)}, f32[8,224,224]{1,2,0:T(8,128)}, u32[]{:S(2)}) copy-start(f32[8,224,224]{1,2,0:T(8,128)} %get-tuple-element.17) | copy-start | bytes 4816900
  180.7 14.1 %all-to-all-start.1 = ((f32[32,2,128]{2,1,0:T(2,128)}), f32[32,2,128]{2,1,0:T(2,128)S(1)}, u32[]{:S(2)}, u32[]{:S(2)}) async-start(f32[32,2,128]{2,1,0:T(2,128)} %broadcast_in_dim.21), calls=%async_computation.1 | async-start | bytes 65536 | tf_op jit(solution)/shard_map/all_to_all | solution.py:78
  187.5 2.6 %copy-start.4 = (bf16[8,28,8,128]{3,2,1,0:T(8,128)(2,1)S(1)}, bf16[8,28,8,128]{3,2,1,0:T(8,128)(2,1)}, u32[]{:S(2)}) copy-start(bf16[8,28,8,128]{3,2,1,0:T(8,128)(2,1)} %fusion.6) | copy-start | bytes 1376260
  195.5 39.0 %all-to-all-start.2 = ((f32[32,2,128]{2,1,0:T(2,128)}), f32[32,2,128]{2,1,0:T(2,128)S(1)}, u32[]{:S(2)}, u32[]{:S(2)}) async-start(f32[32,2,128]{2,1,0:T(2,128)} %broadcast_in_dim.22), calls=%async_computation.2 | async-start | bytes 65536 | tf_op jit(solution)/shard_map/all_to_all | solution.py:78

commit v2 on v1

v2 whole, which is shorter than its diff:
```python
import jax
import jax.numpy as jnp
from jax import lax
from jax.experimental import pallas as pl
from jax.experimental.pallas import tpu as pltpu
from jax.sharding import PartitionSpec as P

HEADS = 8
HEAD = 128
SOURCES = 32
ROWS = 7
SLOTS = 8
TILES = 21
PADDED = SOURCES * SLOTS


def dot(a, b, contract):
    return lax.dot_general(
        a, b, ((contract[:1], contract[1:]), ((), ())), preferred_element_type=jnp.float32
    )


def one_hot(hit):
    return jnp.where(hit, 1.0, 0.0).astype(jnp.bfloat16)


def pack_kernel(plan_ref, query_ref, key_ref, value_ref, out_ref):
    frames = plan_ref.shape[1]
    row = lax.broadcasted_iota(jnp.int32, (PADDED, frames), 0)
    group, slot = row >> 3, row & 7
    plan = jnp.broadcast_to(plan_ref[...], (PADDED, frames))
    pick = one_hot((plan == group * ROWS + slot) & (slot != ROWS))
    spill = value_ref[:, 5 * HEAD :]
    refs = (query_ref, key_ref, value_ref)
    for r in range(ROWS):
        extra = dot(one_hot((plan == group * ROWS + r) & (slot == ROWS)), spill, (1, 0))
        for a in range(3):
            tile = ROWS * a + r
            tensor, head = divmod(tile, HEADS)
            own = dot(pick, refs[tensor][:, head * HEAD : (head + 1) * HEAD], (1, 0))
            both = own + extra[:, a * HEAD : (a + 1) * HEAD]
            out_ref[:, tile] = both.reshape(SOURCES, SLOTS, HEAD).astype(jnp.bfloat16)


def attend_kernel(
    got_ref, segment_ref, grad_ref, query_gain_ref, key_gain_ref,
    query_out, key_out, value_out, part_out,
):
    frames = segment_ref.shape[1]
    scale = HEAD ** (-0.5)
    row = lax.broadcasted_iota(jnp.int32, (PADDED, frames), 0)
    column = lax.broadcasted_iota(jnp.int32, (PADDED, frames), 1)
    hit = (column == row - (row >> 3)) & ((row & 7) != ROWS)
    spread = one_hot(hit)
    segment = jnp.broadcast_to(segment_ref[...], (PADDED, frames)).astype(jnp.float32)
    segment_column = jnp.sum(jnp.where(hit, segment, 0.0), axis=1, keepdims=True)
    pad_column = lax.broadcasted_iota(jnp.int32, (PADDED, 1), 0) & 7
    segment_column = jnp.where(pad_column == ROWS, 9.0, segment_column)
    segment_line = dot(segment[:SLOTS].astype(jnp.bfloat16), spread, (1, 1))[:1]
    pad_line = lax.broadcasted_iota(jnp.int32, (1, PADDED), 1) & 7
    segment_line = jnp.where(pad_line == ROWS, 9.0, segment_line)
    bias = jnp.where(segment_column == segment_line, 0.0, -jnp.inf)

    lane_row = lax.broadcasted_iota(jnp.int32, (SOURCES, SLOTS, HEAD), 1)
    live = lane_row != ROWS

    def tile(index):
        return got_ref[:, index].astype(jnp.float32)

    def own(index):
        return jnp.where(live, tile(index), 0.0).reshape(PADDED, HEAD)

    def spilled(a):
        total = jnp.zeros((SOURCES, SLOTS, HEAD), jnp.float32)
        for r in range(ROWS):
            total = jnp.where(lane_row == r, tile(ROWS * a + r)[:, ROWS:], total)
        return total.reshape(PADDED, HEAD)

    def normalize(raw, gain):
        inverse = lax.rsqrt(jnp.sum(raw * raw, axis=1, keepdims=True) * (1.0 / HEAD) + 1e-06)
        unit = raw * inverse
        return unit, inverse, (unit * gain).astype(jnp.bfloat16)

    def norm_back(d_norm, unit, inverse, gain):
        d_unit = d_norm * gain
        inner = jnp.sum(d_unit * unit, axis=1, keepdims=True) * (1.0 / HEAD)
        return (inverse * (d_unit - unit * inner)).astype(jnp.bfloat16)

    def gather(padded):
        return dot(spread, padded, (0, 0)).astype(jnp.bfloat16)

    query_gain, key_gain = query_gain_ref[...], key_gain_ref[...]
    query_part = jnp.zeros((1, HEAD), jnp.float32)
    key_part = jnp.zeros((1, HEAD), jnp.float32)
    for head in range(HEADS):
        lanes = slice(head * HEAD, (head + 1) * HEAD)
        q_unit, q_inv, q_norm = normalize(own(head), query_gain)
        k_unit, k_inv, k_norm = normalize(own(HEADS + head), key_gain)
        value = own(2 * HEADS + head) if head < 5 else spilled(head - 5)
        value = value.astype(jnp.bfloat16)
        grad_wide = dot(spread, grad_ref[:, lanes], (1, 0))
        grad = grad_wide.astype(jnp.bfloat16)
        scores = dot(q_norm, k_norm, (1, 1)) * scale + bias
        exponent = jnp.exp(scores - jnp.max(scores, axis=1, keepdims=True))
        probs = exponent / jnp.sum(exponent, axis=1, keepdims=True)
        probs_half = probs.astype(jnp.bfloat16)
        output = dot(probs_half, value, (1, 0))
        row_delta = jnp.sum(grad_wide * output, axis=1, keepdims=True)
        value_out[:, lanes] = gather(dot(probs_half, grad, (0, 0)).astype(jnp.bfloat16))
        d_prob = dot(grad, value, (1, 1))
        d_score = (probs * (d_prob - row_delta) * scale).astype(jnp.bfloat16)
        d_qnorm = dot(d_score, k_norm, (1, 0))
        d_knorm = dot(d_score, q_norm, (0, 0))
        query_part += jnp.sum(d_qnorm * q_unit, axis=0, keepdims=True)
        key_part += jnp.sum(d_knorm * k_unit, axis=0, keepdims=True)
        query_out[:, lanes] = gather(norm_back(d_qnorm, q_unit, q_inv, query_gain))
        key_out[:, lanes] = gather(norm_back(d_knorm, k_unit, k_inv, key_gain))
    part_out[:, 0:1, :] = jnp.broadcast_to(query_part[None], (SOURCES, 1, HEAD))
    part_out[:, 1:2, :] = jnp.broadcast_to(key_part[None], (SOURCES, 1, HEAD))


def plane_and_line_groups():
    def flat(x, z_hi, core, y, z_lo):
        return ((x * 4 + z_hi) * 2 + core) * 32 + y * 8 + z_lo

    plane = [
        [flat(x, z_hi, core, y, z_lo) for x in range(4) for y in range(4) for core in range(2)]
        for z_hi in range(4)
        for z_lo in range(8)
    ]
    line = [
        [flat(x, z_hi, core, y, z_lo) for z_hi in range(4) for z_lo in range(8)]
        for x in range(4)
        for y in range(4)
        for core in range(2)
    ]
    return plane, line


def sum_over_all(spread):
    for step, groups in enumerate(plane_and_line_groups()):
        if step:
            spread = jnp.broadcast_to(part, spread.shape)
        spread = lax.all_to_all(
            spread, ("dp", "fsdp"), 0, 0, axis_index_groups=groups, tiled=True
        )
        part = jnp.sum(lax.optimization_barrier(spread), axis=0)
    return part


def on_device(query_in, key_in, value_in, length_plan, segment_ids, out_grad, query_gain, key_gain):
    send = pl.pallas_call(
        pack_kernel,
        out_shape=jax.ShapeDtypeStruct((SOURCES, TILES, SLOTS, HEAD), jnp.bfloat16),
        cost_estimate=pl.CostEstimate(flops=10**9, bytes_accessed=3 * 10**6, transcendentals=0),
        name="pack",
    )(length_plan, query_in, key_in, value_in)
    got = lax.all_to_all(send, "dp", 0, 0, tiled=True)
    like = jax.ShapeDtypeStruct(query_in.shape, jnp.bfloat16)
    query_grad, key_grad, value_grad, parts = pl.pallas_call(
        attend_kernel,
        out_shape=(like, like, like, jax.ShapeDtypeStruct((SOURCES, 2, HEAD), jnp.float32)),
        cost_estimate=pl.CostEstimate(flops=10**9, bytes_accessed=4 * 10**6, transcendentals=10**6),
        name="attend",
    )(got, segment_ids, out_grad, query_gain.reshape(1, HEAD), key_gain.reshape(1, HEAD))
    query_total, key_total = sum_over_all(parts)
    return (query_grad, key_grad, value_grad, query_total, key_total)


def solution(mesh):
    rows = P(("dp", "fsdp"), None)
    return jax.shard_map(
        on_device,
        mesh=mesh,
        in_specs=(rows, rows, rows, rows, rows, rows, P(), P()),
        out_specs=(rows, rows, rows, P(), P()),
        check_vma=False,
    )
```

time: 235 us -> 229 us (0.974)
  blocking collectives: 0 us -> 212 us
  waiting for transfers between devices: 150 us -> 0 us
  starting transfers between devices: 56.3 us -> 0 us
  Pallas kernels: 0 us -> 14.9 us
  matrix products: 9.4 us -> 0 us
  local copies, waits for them, and re-layouts: 9.88 us -> 0.53 us
  other arithmetic: 8.05 us -> 0.09 us
    all_to_all x0 -> x3, blocking collectives: none -> 212 us  [the longest x1 161 us: on_device(): got = lax.all_to_all(send, 'dp', 0, 0, tiled=True)]
    all_to_all x3 -> x0, waiting for transfers between devices: 150 us -> none  [the longest x1 126 us: on_device(): got = lax.all_to_all(jnp.concatenate(sends, axis=1), 'dp', 0, 0, tiled=True)]
    all_to_all x3 -> x0, starting transfers between devices: 56.3 us -> none  [the longest x1 32.6 us: on_device(): got = lax.all_to_all(jnp.concatenate(sends, axis=1), 'dp', 0, 0, tiled=True)]
    pallas_call x0 -> x2, Pallas kernels: none -> 14.9 us  [the longest x1 11 us: on_device(): pl.pallas_call(attend_kernel, out_shape=(like, like, like, jax.ShapeDtype...]
    dot_general x5 -> x0, matrix products: 7.23 us -> none  [the longest x1 2.8 us: attend_heads(): jnp.einsum('hts,thd->shd', probs_half, grad_heads, preferred_element_type...]
    gather x3 -> x0, local copies, waits for them, and re-layouts: 4.75 us -> none  [on_device(): source[inverse].reshape(groups, -1, HEAD)]
    convert_element_type x2 -> x0, other arithmetic: 3.85 us -> none  [norm_back(): return result.reshape(result.shape[0], -1).astype(jnp.bfloat16)]
  transfers between devices with their start and end apart: 3 -> 0, of which waited for: 3 -> 0; matrix products, arithmetic and copies ran while one was open for 2% -> 0% of each run, Pallas kernels for 0% -> 0%
where the time goes in v2:
time: 229 us; the launch traced here: 228 us
  blocking collectives  212 us (93%)
  Pallas kernels  14.9 us (7%)
    all_to_all x1, blocking collectives, on_device(): got = lax.all_to_all(send, 'dp', 0, 0, tiled=True)  161 us
    all_to_all x2, blocking collectives, sum_over_all(): lax.all_to_all(spread, ('dp', 'fsdp'), 0, 0, axis_index_groups=groups, ti...  51.8 us
    pallas_call x1, Pallas kernels, on_device(): pl.pallas_call(attend_kernel, out_shape=(like, like, like, jax.ShapeDtype...  11 us

profile of v2, /device:TPU:1, one launch (start us, length us, event | category | flops | bytes accessed | tf_op | source)
XLA Modules:
  0.0 228.4 jit_solution(2155033215039361739)
XLA Ops:
  0.6 3.8 %pack.1 = bf16[32,21,8,128]{3,2,1,0:T(8,128)(2,1)} custom-call(s32[1,224]{1,0:T(1,128)} %plan_ref.1, bf16[224,1024]{1,0:T(8,128)(2,1)} %query_ref.1, bf16[224,1024]{1,0:T(8,128)(2,1)} %key_ref.1, bf16[224,1024]{1,0:T(8,128)(2,1)} %value_ref.1), custom_call_target="tpu_custom_call" | custom-call | flops 1000000000 | bytes 3000000 | tf_op jit(solution)/shard_map/pack/pallas_call | solution.py:152
  4.5 160.5 %all_to_all.15.got_ref = bf16[32,21,8,128]{3,2,1,0:T(8,128)(2,1)} all-to-all(bf16[32,21,8,128]{3,2,1,0:T(8,128)(2,1)} %pack.1), channel_id=1, replica_groups=mesh['dp'=32,'fsdp'=32] {'dp'}, dimensions={0} | all-to-all | bytes 2752512 | tf_op jit(solution)/shard_map/all_to_all | solution.py:158
  165.0 11.0 %attend.1 = (bf16[224,1024]{1,0:T(8,128)(2,1)}, bf16[224,1024]{1,0:T(8,128)(2,1)}, bf16[224,1024]{1,0:T(8,128)(2,1)}, f32[32,2,128]{2,1,0:T(2,128)}) custom-call(bf16[32,21,8,128]{3,2,1,0:T(8,128)(2,1)} %all_to_all.15.got_ref, s32[1,224]{1,0:T(1,128)} %segment_ref.1, bf16[224,1024]{1,0:T(8,128)(2,1)} %grad_ref.1, f32[1,128]{1,0:T(1,128)} %bitcast.6, ...), custom_call_target="tpu_custom_call" | custom-call | flops 1000000000 | bytes 4000000 | tf_op jit(solution)/shard_map/attend/pallas_call | solution.py:160
  176.0 12.9 %all_to_all.16 = f32[32,2,128]{2,1,0:T(2,128)S(1)} all-to-all(f32[32,2,128]{2,1,0:T(2,128)} %get-tuple-element.12), channel_id=1, replica_groups={{0,32,8,40,16,48,24,56,256,288,264,296,272,304,280,312,512,544,520,552,..., dimensions={0} | all-to-all | bytes 65536 | tf_op jit(solution)/shard_map/all_to_all | solution.py:144
  189.0 38.8 %all_to_all.17 = f32[32,2,128]{2,1,0:T(2,128)S(1)} all-to-all(f32[32,2,128]{2,1,0:T(2,128)S(1)} %broadcast_in_dim.3), channel_id=1, replica_groups={{0,1,2,3,4,5,6,7,64,65,66,67,68,69,70,71,128,129,130,131,132,133,134,13..., dimensions={0} | all-to-all | bytes 65536 | tf_op jit(solution)/shard_map/all_to_all | solution.py:144
  227.9 0.5 slice_bitcast_fusion
  (3 shorter events, 0.1 us)

commit v3 on v2

v3 whole, which is shorter than its diff:
```python
import jax
import jax.numpy as jnp
from jax import lax
from jax.experimental import pallas as pl
from jax.experimental.pallas import tpu as pltpu
from jax.sharding import PartitionSpec as P


HEADS = 8
HEAD = 128
TURNS = 4
PEERS = 8
ROWS = 7
SLOTS = 8
PADDED = TURNS * PEERS * SLOTS
BF16 = jnp.bfloat16

OWN = (
    [(tensor, head) for head in range(5) for tensor in range(3)] + [(0, 5)],
    [(0, 6), (1, 6), (2, 6), (0, 7), (1, 7)],
)
SPILL = (
    [(1, 5, r) for r in range(7)] + [(2, 5, r) for r in range(7)] + [(2, 7, 5), (2, 7, 6)],
    [(2, 7, r) for r in range(5)],
)
CUT = 6 * HEAD


def dot(a, b, contract):
    return lax.dot_general(
        a, b, ((contract[:1], contract[1:]), ((), ())), preferred_element_type=jnp.float32
    )


def one_hot(hit):
    return jnp.where(hit, 1.0, 0.0).astype(BF16)


def place():
    return (lax.axis_index("dp") >> 1) & 3


def pack_kernel(part, plan_ref, query_ref, key_ref, value_ref, *out_refs):
    frames = plan_ref.shape[1]
    row = lax.broadcasted_iota(jnp.int32, (PADDED, frames), 0)
    dest = ((row >> 4) & 3) * 8 + ((place() + (row >> 6)) & 3) * 2 + ((row >> 3) & 1)
    slot = row & 7
    plan = jnp.broadcast_to(plan_ref[...], (PADDED, frames))
    pick = one_hot((plan == dest * ROWS + slot) & (slot != ROWS))
    refs = (query_ref, key_ref, value_ref)
    first = 0 if part == 0 else 6

    def lanes(tensor, head):
        at = (head - first) * HEAD
        return refs[tensor][:, at : at + HEAD]

    by_frame = {}
    for tile, spill in enumerate(SPILL[part]):
        by_frame.setdefault(spill[2], []).append((tile, *spill[:2]))
    for frame, tiles in by_frame.items():
        late = one_hot((plan == dest * ROWS + frame) & (slot == ROWS))
        for tile, tensor, head in tiles:
            both = dot(pick, lanes(*OWN[part][tile]), (1, 0))
            both += dot(late, lanes(tensor, head), (1, 0))
            both = both.reshape(TURNS, PEERS, SLOTS, HEAD).astype(BF16)
            for turn in range(TURNS):
                out_refs[turn][:, tile] = both[turn]


def attend_kernel(part, got_ref, *refs):
    if part == 0:
        segment_ref, grad_ref, query_gain_ref, key_gain_ref = refs[:4]
        outs, (query_pad, key_pad, value_pad, grad_pad) = refs[4:8], refs[8:]
    else:
        rest_ref, before_ref, segment_ref, grad_ref, query_gain_ref, key_gain_ref = refs[:6]
        outs, (query_pad, key_pad, value_pad, grad_pad) = refs[9:13], refs[13:]
    query_out, key_out, value_out, part_out = outs
    frames = segment_ref.shape[1]
    scale = HEAD ** (-0.5)
    exp2_scale = scale * 1.4426950408889634
    here = place()

    def frame_of(row):
        source = (row >> 6) * 8 + ((here - (row >> 3)) & 3) * 2 + ((row >> 5) & 1)
        return jnp.where((row & 7) == ROWS, -1, source * ROWS + (row & 7))

    row = lax.broadcasted_iota(jnp.int32, (PADDED, 1), 0)
    line = lax.broadcasted_iota(jnp.int32, (1, PADDED), 1)
    hit = lax.broadcasted_iota(jnp.int32, (PADDED, frames), 1) == frame_of(row)
    spread = one_hot(hit)
    gather = one_hot(lax.broadcasted_iota(jnp.int32, (frames, PADDED), 0) == frame_of(line))
    segment = jnp.broadcast_to(segment_ref[...], (PADDED, frames)).astype(jnp.float32)
    segment_row = jnp.sum(jnp.where(hit, segment, 0.0), axis=1, keepdims=True)
    segment_row = jnp.where((row & 7) == ROWS, 9.0, segment_row)
    segment_line = dot(segment[:SLOTS].astype(BF16), spread, (1, 1))[:1]
    segment_line = jnp.where((line & 7) == ROWS, 9.0, segment_line)
    bias = jnp.where(segment_row == segment_line, 0.0, -jnp.inf)
    grad_pad[...] = dot(spread, grad_ref[...], (1, 0)).astype(BF16)
    slot = lax.broadcasted_iota(jnp.int32, (PEERS, TURNS, SLOTS, HEAD), 2)

    def fetch(tensor, head):
        if (tensor, head) in OWN[part]:
            return got_ref[:, :, OWN[part].index((tensor, head))].reshape(PADDED, HEAD)
        total = None
        for r in range(ROWS):
            if (tensor, head, r) in SPILL[part]:
                tile = got_ref[:, :, SPILL[part].index((tensor, head, r))]
            else:
                tile = rest_ref[:, :, SPILL[0].index((tensor, head, r)) - 14]
            spilled = jnp.broadcast_to(tile.astype(jnp.float32)[:, :, ROWS:], slot.shape)
            total = spilled if total is None else jnp.where(slot == r, spilled, total)
        return total.reshape(PADDED, HEAD).astype(BF16)

    def normalize(raw, gain):
        raw = raw.astype(jnp.float32)
        inverse = lax.rsqrt(jnp.sum(raw * raw, axis=1, keepdims=True) * (1.0 / HEAD) + 1e-06)
        unit = raw * inverse
        return unit, inverse, (unit * gain).astype(BF16)

    def norm_back(d_norm, unit, inverse, gain):
        d_unit = d_norm * gain
        inner = jnp.sum(d_unit * unit, axis=1, keepdims=True) * (1.0 / HEAD)
        return (inverse * (d_unit - unit * inner)).astype(BF16)

    query_gain, key_gain = query_gain_ref[...], key_gain_ref[...]
    query_part = jnp.zeros((1, HEAD), jnp.float32)
    key_part = jnp.zeros((1, HEAD), jnp.float32)
    first, last = (0, 6) if part == 0 else (6, HEADS)
    for head in range(first, last):
        lanes = slice((head - first) * HEAD, (head - first + 1) * HEAD)
        q_unit, q_inv, q_norm = normalize(fetch(0, head), query_gain)
        k_unit, k_inv, k_norm = normalize(fetch(1, head), key_gain)
        value = fetch(2, head)
        grad = grad_pad[:, lanes]
        halves, scores_grad = [], []
        for start in range(0, PADDED, HEAD):
            block = slice(start, start + HEAD)
            scores = dot(k_norm, q_norm[block], (1, 1)) + bias[:, block]
            scores = (scores - jnp.max(scores, axis=0, keepdims=True)) * exp2_scale
            exponent = jnp.exp2(scores)
            probs = exponent * (1.0 / jnp.sum(exponent, axis=0, keepdims=True))
            half = probs.astype(BF16)
            d_prob = dot(value, grad[block], (1, 1))
            row_delta = jnp.sum(half.astype(jnp.float32) * d_prob, axis=0, keepdims=True)
            d_score = (probs * (d_prob - row_delta) * scale).astype(BF16)
            halves.append(half)
            scores_grad.append(d_score)
        probs_half = jnp.concatenate(halves, axis=1)
        d_score = jnp.concatenate(scores_grad, axis=1)
        value_pad[:, lanes] = dot(probs_half, grad, (1, 0)).astype(BF16)
        d_qnorm = dot(d_score, k_norm, (0, 0))
        d_knorm = dot(d_score, q_norm, (1, 0))
        query_part += jnp.sum(d_qnorm * q_unit, axis=0, keepdims=True)
        key_part += jnp.sum(d_knorm * k_unit, axis=0, keepdims=True)
        query_pad[:, lanes] = norm_back(d_qnorm, q_unit, q_inv, query_gain)
        key_pad[:, lanes] = norm_back(d_knorm, k_unit, k_inv, key_gain)
    parts = jnp.concatenate([query_part, key_part], axis=0)
    if part == 0:
        part_out[...] = parts
    else:
        part_out[...] = jnp.broadcast_to((before_ref[...] + parts)[None], part_out.shape)
    for padded, out in ((query_pad, query_out), (key_pad, key_out), (value_pad, value_out)):
        out[...] = dot(gather, padded[...], (1, 0)).astype(BF16)


def whole(shape):
    return pl.BlockSpec(shape, lambda i: (0,) * len(shape))


def lane_block(part):
    return pl.BlockSpec((224, CUT), lambda i: (0, 0)) if part == 0 else pl.BlockSpec(
        (224, HEADS * HEAD - CUT), lambda i: (0, 3)
    )


def pack_call(part, plan, query_in, key_in, value_in):
    tiles = len(OWN[part])
    shape = (PEERS, tiles, SLOTS, HEAD)
    value_block = whole(value_in.shape) if part == 0 else lane_block(1)
    return pl.pallas_call(
        lambda *refs: pack_kernel(part, *refs),
        grid=(1,),
        in_specs=[whole(plan.shape), lane_block(part), lane_block(part), value_block],
        out_specs=[whole(shape)] * TURNS,
        out_shape=[jax.ShapeDtypeStruct(shape, BF16)] * TURNS,
        cost_estimate=pl.CostEstimate(
            flops=5 * 10**7 * tiles, bytes_accessed=13 * 10**4 * tiles, transcendentals=0
        ),
    )(plan, query_in, key_in, value_in)


def attend_call(part, got, before, segment_ids, out_grad, query_gain, key_gain):
    like = jax.ShapeDtypeStruct(out_grad.shape, BF16)
    heads = 6 if part == 0 else 2
    padded = pltpu.VMEM((PADDED, heads * HEAD), BF16)
    args = [got]
    specs = [whole(got.shape)]
    part_shape = (2, HEAD) if part == 0 else (TURNS * PEERS, 2, HEAD)
    aliases = {}
    if part == 1:
        got_before, *grads, parts = before
        args += [got_before, parts]
        specs += [
            pl.BlockSpec((PEERS, TURNS, 2, SLOTS, HEAD), lambda i: (0, 0, 7, 0, 0)),
            whole(parts.shape),
        ]
    args += [segment_ids, out_grad, query_gain.reshape(1, HEAD), key_gain.reshape(1, HEAD)]
    specs += [whole(segment_ids.shape), lane_block(part), whole((1, HEAD)), whole((1, HEAD))]
    if part == 1:
        aliases = {len(args) + i: i for i in range(3)}
        args += grads
        specs += [pl.BlockSpec(memory_space=pl.ANY)] * 3
    return pl.pallas_call(
        lambda *refs: attend_kernel(part, *refs),
        grid=(1,),
        in_specs=specs,
        out_specs=[lane_block(part)] * 3 + [whole(part_shape)],
        out_shape=[like, like, like, jax.ShapeDtypeStruct(part_shape, jnp.float32)],
        scratch_shapes=[padded] * 4,
        input_output_aliases=aliases,
        cost_estimate=pl.CostEstimate(
            flops=10**8 * heads, bytes_accessed=5 * 10**5 * heads, transcendentals=10**5 * heads
        ),
    )(*args)


def index(x, z_hi, core):
    return (x * 4 + z_hi) * 2 + core


def turn_by(turn, data):
    pairs = [
        (index(x, z, core), index(x, (z + turn) % TURNS, core))
        for x in range(4)
        for z in range(TURNS)
        for core in range(2)
    ]
    return lax.ppermute(data, "dp", pairs)


def among_peers(data):
    groups = [[index(x, z, core) for x in range(4) for core in range(2)] for z in range(TURNS)]
    return lax.all_to_all(data, "dp", 0, 0, axis_index_groups=groups, tiled=True)


def plane_and_line_groups():
    def flat(x, z_hi, core, y, z_lo):
        return index(x, z_hi, core) * 32 + y * 8 + z_lo

    plane = [
        [flat(x, z_hi, core, y, z_lo) for x in range(4) for y in range(4) for core in range(2)]
        for z_hi in range(4)
        for z_lo in range(8)
    ]
    line = [
        [flat(x, z_hi, core, y, z_lo) for z_hi in range(4) for z_lo in range(8)]
        for x in range(4)
        for y in range(4)
        for core in range(2)
    ]
    return plane, line


def sum_over_all(spread):
    for step, groups in enumerate(plane_and_line_groups()):
        if step:
            spread = jnp.broadcast_to(part, spread.shape)
        spread = lax.all_to_all(
            spread, ("dp", "fsdp"), 0, 0, axis_index_groups=groups, tiled=True
        )
        part = jnp.sum(lax.optimization_barrier(spread), axis=0)
    return part


def on_device(query_in, key_in, value_in, length_plan, segment_ids, out_grad, query_gain, key_gain):
    moved = []
    for part in range(2):
        own, *sends = pack_call(part, length_plan, query_in, key_in, value_in)
        arrived = [own, None, None, None]
        for turn in (1, 3, 2):
            arrived[turn] = turn_by(turn, sends[turn - 1])
        moved.append(arrived)
    shared = (segment_ids, out_grad, query_gain, key_gain)
    got = among_peers(jnp.stack(moved[0], axis=1))
    first = attend_call(0, got, None, *shared)
    last, first = lax.optimization_barrier((moved[1], first))
    got_last = among_peers(jnp.stack(last, axis=1))
    *grads, parts = attend_call(1, got_last, [got, *first], *shared)
    query_total, key_total = sum_over_all(parts)
    return (*grads, query_total, key_total)


def solution(mesh):
    rows = P(("dp", "fsdp"), None)
    return jax.shard_map(
        on_device,
        mesh=mesh,
        in_specs=(rows, rows, rows, rows, rows, rows, P(), P()),
        out_specs=(rows, rows, rows, P(), P()),
        check_vma=False,
    )
```

time: 229 us -> 245 us (1.070)
  blocking collectives: 212 us -> 64.4 us
  starting transfers between devices: 0 us -> 81.3 us
  waiting for transfers between devices: 0 us -> 79 us
    all_to_all x1, blocking collectives: 161 us -> 12.5 us  [among_peers(): lax.all_to_all(data, 'dp', 0, 0, axis_index_groups=groups, tiled=True)]
    ppermute x0 -> x6, waiting for transfers between devices: none -> 79 us  [turn_by(): return lax.ppermute(data, 'dp', pairs)]
    ppermute x0 -> x6, starting transfers between devices: none -> 76.7 us  [turn_by(): return lax.ppermute(data, 'dp', pairs)]
    all_to_all x0 -> x1, starting transfers between devices: none -> 4.62 us  [among_peers(): lax.all_to_all(data, 'dp', 0, 0, axis_index_groups=groups, tiled=True)]
    pallas_call x2 -> x4, Pallas kernels: 14.9 us -> 15 us  [the longest x2 9.31 us: attend_call(): pl.pallas_call(lambda *refs: attend_kernel(part, *refs), grid=(1,), in_sp...]
  transfers between devices with their start and end apart: 0 -> 7, of which waited for: 0 -> 3; matrix products, arithmetic and copies ran while one was open for 0% -> 0% of each run, Pallas kernels for 0% -> 3%
where the time goes in v3:
time: 245 us; the launch traced here: 244 us
  starting transfers between devices  81.3 us (33%)
  waiting for transfers between devices  79 us (32%)
  blocking collectives  64.4 us (26%)
  Pallas kernels  15 us (6%)
    ppermute x6, waiting for transfers between devices, turn_by(): return lax.ppermute(data, 'dp', pairs)  79 us
    ppermute x6, starting transfers between devices, turn_by(): return lax.ppermute(data, 'dp', pairs)  76.7 us
    all_to_all x2, blocking collectives, sum_over_all(): lax.all_to_all(spread, ('dp', 'fsdp'), 0, 0, axis_index_groups=groups, ti...  51.8 us
    all_to_all x1, blocking collectives, among_peers(): lax.all_to_all(data, 'dp', 0, 0, axis_index_groups=groups, tiled=True)  12.5 us
    pallas_call x2, Pallas kernels, attend_call(): pl.pallas_call(lambda *refs: attend_kernel(part, *refs), grid=(1,), in_sp...  9.31 us
    pallas_call x2, Pallas kernels, pack_call(): pl.pallas_call(lambda *refs: pack_kernel(part, *refs), grid=(1,), in_spec...  5.71 us
  transfers between devices with their start and end apart: 7, of which 3 were waited for; matrix products, arithmetic and copies ran while one was open for 0% of the time, Pallas kernels for 3%

profile of v3, /device:TPU:1, one launch (start us, length us, event | category | flops | bytes accessed | tf_op | source)
XLA Modules:
  0.0 244.1 jit_solution(5968893770460734001)
XLA Ops:
  0.6 3.4 %shard_map.120 = (bf16[8,16,8,128]{3,2,1,0:T(8,128)(2,1)}, bf16[8,16,8,128]{3,2,1,0:T(8,128)(2,1)}, bf16[8,16,8,128]{3,2,1,0:T(8,128)(2,1)}, bf16[8,16,8,128]{3,2,1,0:T(8,128)(2,1)}) custom-call(s32[1,224]{1,0:T(1,128)} %refs_0_.3, bf16[224,1024]{1,0:T(8,128)(2,1)} %refs_1_.4, bf16[224,1024]{1,0:T(8,128)(2,1)} %refs_2_.4, bf16[224,1024]{1,0:T(8,128)(2,1)} %refs_3_.4), custom_call_target="tpu_custom_call" | custom-call | flops 800000000 | bytes 2080000 | tf_op jit(solution)/shard_map/pallas_call | solution.py:180
  4.1 16.2 %collective-permute-start.3 = (bf16[8,16,8,128]{3,2,1,0:T(8,128)(2,1)}, bf16[8,16,8,128]{3,2,1,0:T(8,128)(2,1)S(1)}, u32[]{:S(2)}, u32[]{:S(2)}) collective-permute-start(bf16[8,16,8,128]{3,2,1,0:T(8,128)(2,1)} %get-tuple-element.34), channel_id=1, source_target_pairs={{0,64},{32,96},{64,128},{96,160},{128,192},{160,224},{192,0},{224,... | collective-permute-start | bytes 786440 | tf_op jit(solution)/shard_map/ppermute | solution.py:238
  20.3 19.1 %collective-permute-start.4 = (bf16[8,16,8,128]{3,2,1,0:T(8,128)(2,1)}, bf16[8,16,8,128]{3,2,1,0:T(8,128)(2,1)S(1)}, u32[]{:S(2)}, u32[]{:S(2)}) collective-permute-start(bf16[8,16,8,128]{3,2,1,0:T(8,128)(2,1)} %get-tuple-element.35), channel_id=1, source_target_pairs={{0,128},{32,160},{64,192},{96,224},{128,0},{160,32},{192,64},{224,... | collective-permute-start | bytes 786440 | tf_op jit(solution)/shard_map/ppermute | solution.py:238
  39.4 8.2 %collective-permute-start.5 = (bf16[8,16,8,128]{3,2,1,0:T(8,128)(2,1)}, bf16[8,16,8,128]{3,2,1,0:T(8,128)(2,1)S(1)}, u32[]{:S(2)}, u32[]{:S(2)}) collective-permute-start(bf16[8,16,8,128]{3,2,1,0:T(8,128)(2,1)} %get-tuple-element.36), channel_id=1, source_target_pairs={{0,192},{32,224},{64,0},{96,32},{128,64},{160,96},{192,128},{224,1... | collective-permute-start | bytes 786440 | tf_op jit(solution)/shard_map/ppermute | solution.py:238
  47.6 0.0 collective-permute-done.3
  47.6 63.3 %collective-permute-done.4 = bf16[8,16,8,128]{3,2,1,0:T(8,128)(2,1)S(1)} collective-permute-done((bf16[8,16,8,128]{3,2,1,0:T(8,128)(2,1)}, bf16[8,16,8,128]{3,2,1,0:T(8,128)(2,1)S(1)}, u32[]{:S(2)}, u32[]{:S(2)}) %collective-permute-start.4) | collective-permute-done | bytes 262176 | tf_op jit(solution)/shard_map/ppermute | solution.py:238
  110.9 12.2 %collective-permute-done.5 = bf16[8,16,8,128]{3,2,1,0:T(8,128)(2,1)S(1)} collective-permute-done((bf16[8,16,8,128]{3,2,1,0:T(8,128)(2,1)}, bf16[8,16,8,128]{3,2,1,0:T(8,128)(2,1)S(1)}, u32[]{:S(2)}, u32[]{:S(2)}) %collective-permute-start.5) | collective-permute-done | bytes 262176 | tf_op jit(solution)/shard_map/ppermute | solution.py:238
  123.2 2.0 pad_maximum_fusion
  125.2 4.6 %all-to-all-start = ((bf16[8,4,16,8,128]{4,3,2,1,0:T(8,128)(2,1)}), bf16[8,4,16,8,128]{4,3,2,1,0:T(8,128)(2,1)S(1)}, u32[]{:S(2)}, u32[]{:S(2)}) async-start(bf16[8,4,16,8,128]{4,3,2,1,0:T(8,128)(2,1)} %pad_maximum_fusion), calls=%async_computation | async-start | bytes 2097152 | tf_op jit(solution)/shard_map/all_to_all | solution.py:243
  129.8 2.3 shard_map.119
  132.1 5.5 %collective-permute-start = (bf16[8,5,8,128]{3,2,1,0:T(8,128)(2,1)}, bf16[8,5,8,128]{3,2,1,0:T(8,128)(2,1)S(1)}, u32[]{:S(2)}, u32[]{:S(2)}) collective-permute-start(bf16[8,5,8,128]{3,2,1,0:T(8,128)(2,1)} %get-tuple-element.30), channel_id=1, source_target_pairs={{0,64},{32,96},{64,128},{96,160},{128,192},{160,224},{192,0},{224,... | collective-permute-start | bytes 245768 | tf_op jit(solution)/shard_map/ppermute | solution.py:238
  137.6 19.6 %collective-permute-start.1 = (bf16[8,5,8,128]{3,2,1,0:T(8,128)(2,1)}, bf16[8,5,8,128]{3,2,1,0:T(8,128)(2,1)S(1)}, u32[]{:S(2)}, u32[]{:S(2)}) collective-permute-start(bf16[8,5,8,128]{3,2,1,0:T(8,128)(2,1)} %get-tuple-element.31), channel_id=1, source_target_pairs={{0,128},{32,160},{64,192},{96,224},{128,0},{160,32},{192,64},{224,... | collective-permute-start | bytes 245768 | tf_op jit(solution)/shard_map/ppermute | solution.py:238
  157.2 8.1 %collective-permute-start.2 = (bf16[8,5,8,128]{3,2,1,0:T(8,128)(2,1)}, bf16[8,5,8,128]{3,2,1,0:T(8,128)(2,1)S(1)}, u32[]{:S(2)}, u32[]{:S(2)}) collective-permute-start(bf16[8,5,8,128]{3,2,1,0:T(8,128)(2,1)} %get-tuple-element.32), channel_id=1, source_target_pairs={{0,192},{32,224},{64,0},{96,32},{128,64},{160,96},{192,128},{224,1... | collective-permute-start | bytes 245768 | tf_op jit(solution)/shard_map/ppermute | solution.py:238
  165.3 0.0 all-to-all-done.refs_0_.refs_1_
  165.3 0.0 copy-start
  165.4 1.0 copy-done
  166.3 0.0 copy-start.1
  166.3 6.0 %shard_map.121 = (bf16[224,1024]{1,0:T(8,128)(2,1)}, bf16[224,1024]{1,0:T(8,128)(2,1)}, bf16[224,1024]{1,0:T(8,128)(2,1)}, f32[2,128]{1,0:T(2,128)}) custom-call(bf16[8,4,16,8,128]{4,3,2,1,0:T(8,128)(2,1)} %copy-done, s32[1,224]{1,0:T(1,128)} %refs_3_.5, bf16[224,1024]{1,0:T(8,128)(2,1)} %refs_4_.1, f32[1,128]{1,0:T(1,128)} %bitcast.22, f32[1,128]{1,0:T(1,128)} %bitcast.24), custom_call_target="tpu_custom_call" | custom-call | flops 600000000 | bytes 3000000 | tf_op jit(solution)/shard_map/pallas_call | solution.py:213
  172.3 0.0 collective-permute-done
  172.3 0.0 collective-permute-done.1
  172.3 3.4 %collective-permute-done.2 = bf16[8,5,8,128]{3,2,1,0:T(8,128)(2,1)S(1)} collective-permute-done((bf16[8,5,8,128]{3,2,1,0:T(8,128)(2,1)}, bf16[8,5,8,128]{3,2,1,0:T(8,128)(2,1)S(1)}, u32[]{:S(2)}, u32[]{:S(2)}) %collective-permute-start.2) | collective-permute-done | bytes 81952 | tf_op jit(solution)/shard_map/ppermute | solution.py:238
  175.7 0.0 copy-done.1
  175.8 12.5 %all_to_all.20.refs_0_ = bf16[8,4,5,8,128]{4,3,2,1,0:T(8,128)(2,1)} all-to-all(bf16[8,4,5,8,128]{4,3,2,1,0:T(8,128)(2,1)S(1)} %pad_maximum_fusion.1), channel_id=1, replica_groups={{0,32,256,288,512,544,768,800},{64,96,320,352,576,608,832,864},{128,160..., dimensions={0} | all-to-all | bytes 655360 | tf_op jit(solution)/shard_map/all_to_all | solution.py:243
  188.3 3.3 %shard_map.122 = (bf16[224,1024]{1,0:T(8,128)(2,1)}, bf16[224,1024]{1,0:T(8,128)(2,1)}, bf16[224,1024]{1,0:T(8,128)(2,1)}, f32[32,2,128]{2,1,0:T(2,128)}) custom-call(bf16[8,4,5,8,128]{4,3,2,1,0:T(8,128)(2,1)} %all_to_all.20.refs_0_, bf16[8,4,16,8,128]{4,3,2,1,0:T(8,128)(2,1)} %copy-done, ...), custom_call_target="tpu_custom_call", output_to_operand_aliasing={{0}: (7, {}), {1}: (8, {}), {2}: (9, {})} | custom-call | flops 200000000 | bytes 1000000 | tf_op jit(solution)/shard_map/pallas_call | solution.py:213
  191.6 13.5 %all_to_all.21 = f32[32,2,128]{2,1,0:T(2,128)S(1)} all-to-all(f32[32,2,128]{2,1,0:T(2,128)} %get-tuple-element.52), channel_id=1, replica_groups={{0,32,8,40,16,48,24,56,256,288,264,296,272,304,280,312,512,544,520,552,..., dimensions={0} | all-to-all | bytes 65536 | tf_op jit(solution)/shard_map/all_to_all | solution.py:268
  205.2 38.3 %all_to_all.22 = f32[32,2,128]{2,1,0:T(2,128)S(1)} all-to-all(f32[32,2,128]{2,1,0:T(2,128)S(1)} %broadcast_in_dim.3), channel_id=1, replica_groups={{0,1,2,3,4,5,6,7,64,65,66,67,68,69,70,71,128,129,130,131,132,133,134,13..., dimensions={0} | all-to-all | bytes 65536 | tf_op jit(solution)/shard_map/all_to_all | solution.py:268
  243.6 0.5 slice_bitcast_fusion
  (4 shorter events, 0.1 us)
Async XLA Ops:
  4.1 43.5 %collective-permute-start.3 = (bf16[8,16,8,128]{3,2,1,0:T(8,128)(2,1)}, bf16[8,16,8,128]{3,2,1,0:T(8,128)(2,1)S(1)}, u32[]{:S(2)}, u32[]{:S(2)}) collective-permute-start(bf16[8,16,8,128]{3,2,1,0:T(8,128)(2,1)} %get-tuple-element.34), channel_id=1, source_target_pairs={{0,64},{32,96},{64,128},{96,160},{128,192},{160,224},{192,0},{224,... | collective-permute-start | bytes 786440 | tf_op jit(solution)/shard_map/ppermute | solution.py:238
  20.3 90.6 %collective-permute-start.4 = (bf16[8,16,8,128]{3,2,1,0:T(8,128)(2,1)}, bf16[8,16,8,128]{3,2,1,0:T(8,128)(2,1)S(1)}, u32[]{:S(2)}, u32[]{:S(2)}) collective-permute-start(bf16[8,16,8,128]{3,2,1,0:T(8,128)(2,1)} %get-tuple-element.35), channel_id=1, source_target_pairs={{0,128},{32,160},{64,192},{96,224},{128,0},{160,32},{192,64},{224,... | collective-permute-start | bytes 786440 | tf_op jit(solution)/shard_map/ppermute | solution.py:238
  39.4 83.7 %collective-permute-start.5 = (bf16[8,16,8,128]{3,2,1,0:T(8,128)(2,1)}, bf16[8,16,8,128]{3,2,1,0:T(8,128)(2,1)S(1)}, u32[]{:S(2)}, u32[]{:S(2)}) collective-permute-start(bf16[8,16,8,128]{3,2,1,0:T(8,128)(2,1)} %get-tuple-element.36), channel_id=1, source_target_pairs={{0,192},{32,224},{64,0},{96,32},{128,64},{160,96},{192,128},{224,1... | collective-permute-start | bytes 786440 | tf_op jit(solution)/shard_map/ppermute | solution.py:238
  125.2 40.1 %all-to-all-start = ((bf16[8,4,16,8,128]{4,3,2,1,0:T(8,128)(2,1)}), bf16[8,4,16,8,128]{4,3,2,1,0:T(8,128)(2,1)S(1)}, u32[]{:S(2)}, u32[]{:S(2)}) async-start(bf16[8,4,16,8,128]{4,3,2,1,0:T(8,128)(2,1)} %pad_maximum_fusion), calls=%async_computation | async-start | bytes 2097152 | tf_op jit(solution)/shard_map/all_to_all | solution.py:243
  132.1 40.2 %collective-permute-start = (bf16[8,5,8,128]{3,2,1,0:T(8,128)(2,1)}, bf16[8,5,8,128]{3,2,1,0:T(8,128)(2,1)S(1)}, u32[]{:S(2)}, u32[]{:S(2)}) collective-permute-start(bf16[8,5,8,128]{3,2,1,0:T(8,128)(2,1)} %get-tuple-element.30), channel_id=1, source_target_pairs={{0,64},{32,96},{64,128},{96,160},{128,192},{160,224},{192,0},{224,... | collective-permute-start | bytes 245768 | tf_op jit(solution)/shard_map/ppermute | solution.py:238
  137.6 34.7 %collective-permute-start.1 = (bf16[8,5,8,128]{3,2,1,0:T(8,128)(2,1)}, bf16[8,5,8,128]{3,2,1,0:T(8,128)(2,1)S(1)}, u32[]{:S(2)}, u32[]{:S(2)}) collective-permute-start(bf16[8,5,8,128]{3,2,1,0:T(8,128)(2,1)} %get-tuple-element.31), channel_id=1, source_target_pairs={{0,128},{32,160},{64,192},{96,224},{128,0},{160,32},{192,64},{224,... | collective-permute-start | bytes 245768 | tf_op jit(solution)/shard_map/ppermute | solution.py:238
  157.2 18.5 %collective-permute-start.2 = (bf16[8,5,8,128]{3,2,1,0:T(8,128)(2,1)}, bf16[8,5,8,128]{3,2,1,0:T(8,128)(2,1)S(1)}, u32[]{:S(2)}, u32[]{:S(2)}) collective-permute-start(bf16[8,5,8,128]{3,2,1,0:T(8,128)(2,1)} %get-tuple-element.32), channel_id=1, source_target_pairs={{0,192},{32,224},{64,0},{96,32},{128,64},{160,96},{192,128},{224,1... | collective-permute-start | bytes 245768 | tf_op jit(solution)/shard_map/ppermute | solution.py:238
  165.3 1.0 copy-start
  166.3 9.4 %copy-start.1 = (bf16[8,5,8,128]{3,2,1,0:T(8,128)(2,1)S(1)}, bf16[8,5,8,128]{3,2,1,0:T(8,128)(2,1)}, u32[]{:S(2)}) copy-start(bf16[8,5,8,128]{3,2,1,0:T(8,128)(2,1)} %get-tuple-element.41) | copy-start | bytes 245764
